TPU v7x, 32 devices: a whole 2x2x4 slice. The times are simulated.
32 devices in a mesh: gx: 8 (over y, x, core), gy: 4 (over z).
Axes of the slice: x: 2, y: 2, z: 4, core: 2. Of those that a mesh axis runs over, the one named last changes fastest.
Arguments:
- tokens: bfloat16 [3072, 2048], P('gx', 'gy'), may hold values from -40 to 40
- gain: float32 [2048], replicated, may hold values from 0.1 to 1.9
- w_qkv: bfloat16 [2048, 3, 16, 128], P('gx', None, 'gy'), may hold values from -0.176776695 to 0.176776695
- w_out: bfloat16 [2048, 2048], P('gx', 'gy'), may hold values from -0.125 to 0.125
- lengths: int32 [6], replicated, may hold values from 1 to 2048, 3072 in all
Outputs:
- mixed: bfloat16 [3072, 2048], P('gx', 'gy')
- key_cache: bfloat16 [3072, 16, 128], P('gx', 'gy')
- value_cache: bfloat16 [3072, 16, 128], P('gx', 'gy')
Inputs may be any that keep to these rules, and one draw needn't show every extreme that they name: lengths are positive and sum to 3072; the longest is exactly 2048.
All inputs are finite; a program needn't handle non-finite values.
Results may differ from a plain program's by a relative error of at most 0.012.
The roundings to bfloat16 on the way count: a program that leaves them out, or rounds other values in their place, can miss the bound.
Values may be sent and summed in bfloat16 or wider, within the bound.
No kernel may reach another device: no remote copies, remote signals or barrier semaphores. Data moves between devices by JAX's collectives and lax.ppermute only.
A program may use at most 64 MiB of HBM per device.

v0:
```python
import math
import jax
import jax.numpy as jnp
from jax import lax
from jax.sharding import PartitionSpec as P


def rotate(vectors, position):
    half = vectors.shape[-1] // 2
    freq = 10000.0 ** (-(2.0 * jnp.arange(half, dtype=jnp.float32)) / vectors.shape[-1])
    angle = position.astype(jnp.float32)[:, None, None] * freq[None, None, :]
    cosine = jnp.cos(angle)
    sine = jnp.sin(angle)
    first = vectors[..., :half]
    second = vectors[..., half:]
    return jnp.concatenate(
        [first * cosine - second * sine, second * cosine + first * sine], axis=-1
    )


def block_rows(count):
    size = count
    while size > 1024 and size % 2 == 0:
        size = size // 2
    return size


def local(tokens, gain, w_qkv, w_out, lengths):
    tok_dev = tokens.shape[0]
    hloc = w_qkv.shape[2]
    hsize = w_qkv.shape[3]
    whole = lax.all_gather(tokens, "gy", axis=1, tiled=True)
    wide = whole.astype(jnp.float32)
    meansq = jnp.mean(wide * wide, axis=-1, keepdims=True)
    normed = (wide * lax.rsqrt(meansq + 1e-06) * gain[None, :]).astype(jnp.bfloat16)
    piece = lax.all_gather(w_qkv, "gx", axis=0, tiled=True)
    columns = normed
    projected = jnp.dot(
        columns, piece.reshape(piece.shape[0], -1), preferred_element_type=jnp.float32
    )
    projected = projected.reshape(tok_dev, 3, hloc, hsize)
    mine = lax.axis_index("gx")
    glob = mine * tok_dev + jnp.arange(tok_dev, dtype=jnp.int32)
    doc_start = jnp.cumsum(lengths) - lengths
    begin = jnp.max(jnp.where(doc_start[None, :] <= glob[:, None], doc_start[None, :], 0), axis=1)
    position = glob - begin
    query = rotate(projected[:, 0], position).astype(jnp.bfloat16)
    keys_own = rotate(projected[:, 1], position).astype(jnp.bfloat16)
    vals_own = projected[:, 2].astype(jnp.bfloat16)
    scale = 1.0 / math.sqrt(hsize)

    def tile_step(state, keys_blk, vals_blk, first):
        running, totals, accum = state
        kidx = first + jnp.arange(keys_blk.shape[0], dtype=jnp.int32)
        score = (
            jnp.einsum("qhd,khd->hqk", query, keys_blk, preferred_element_type=jnp.float32) * scale
        )
        keep = (kidx[None, :] >= begin[:, None]) & (kidx[None, :] <= glob[:, None])
        score = jnp.where(keep[None], score, -1e30)
        newmax = jnp.maximum(running, jnp.max(score, axis=-1))
        weight = jnp.where(keep[None], jnp.exp(score - newmax[..., None]), 0.0)
        factor = jnp.exp(running - newmax)
        totals = totals * factor + jnp.sum(weight, axis=-1)
        update = jnp.einsum(
            "hqk,khd->hqd",
            weight.astype(jnp.bfloat16),
            vals_blk,
            preferred_element_type=jnp.float32,
        )
        accum = accum * factor[..., None] + update
        return (newmax, totals, accum)

    initial = (
        jnp.full((hloc, tok_dev), -1e30, jnp.float32),
        jnp.zeros((hloc, tok_dev), jnp.float32),
        jnp.zeros((hloc, tok_dev, hsize), jnp.float32),
    )
    keys_piece = lax.all_gather(keys_own, "gx", axis=0, tiled=True)
    vals_piece = lax.all_gather(vals_own, "gx", axis=0, tiled=True)
    count = keys_piece.shape[0]
    size = block_rows(count)

    def one_tile(number, inner):
        first = (number * size).astype(jnp.int32)
        keys_blk = lax.dynamic_slice_in_dim(keys_piece, first, size, 0)
        vals_blk = lax.dynamic_slice_in_dim(vals_piece, first, size, 0)
        return tile_step(inner, keys_blk, vals_blk, first)

    running, totals, accum = lax.fori_loop(0, count // size, one_tile, initial)
    attended = (accum / totals[..., None]).astype(jnp.bfloat16)
    attended = jnp.transpose(attended, (1, 0, 2)).reshape(tok_dev, hloc * hsize)
    all_heads = lax.all_gather(attended, "gy", axis=1, tiled=True)
    columns = all_heads
    mixed = jnp.dot(
        columns, lax.all_gather(w_out, "gx", axis=0, tiled=True), preferred_element_type=jnp.float32
    ).astype(jnp.bfloat16)
    return (mixed, keys_own, vals_own)


def solution(mesh):
    return jax.shard_map(
        local,
        mesh=mesh,
        in_specs=(P("gx", "gy"), P(), P("gx", None, "gy", None), P("gx", "gy"), P()),
        out_specs=(P("gx", "gy"), P("gx", "gy", None), P("gx", "gy", None)),
        check_vma=False,
    )
```

profile of v0, /device:TPU:0, one launch (start us, length us, event | category | flops | bytes accessed | tf_op | source)
XLA Modules:
  0.0 282.4 jit_solution(10697021689812042305)
XLA Ops:
  7.2 0.7 all-gather.8.cloned.1.call-update
  7.9 0.7 all-gather.10.cloned.1.call-update
  8.7 0.8 reduce-window.9
  9.5 0.7 bitcast_subtract_fusion
  10.7 38.7 %all-gather.8.cloned.1.call-done = bf16[384,2048]{1,0:T(8,128)(2,1)} async-done(((bf16[384,512]{1,0:T(8,128)(2,1)}), bf16[384,2048]{1,0:T(8,128)(2,1)}) %all-gather.8.cloned.1.call-update) | async-done | bytes 1572880 | tf_op jit(solution)/shard_map/all_gather | solution.py:32
  49.4 1.8 fusion.22
  51.2 44.5 %all-gather.10.cloned.1.call-done = bf16[2048,3,4,128]{3,2,1,0:T(4,128)(2,1)} async-done(((bf16[256,3,4,128]{3,2,1,0:T(4,128)(2,1)}), bf16[2048,3,4,128]{3,2,1,0:T(4,128)(2,1)}) %all-gather.10.cloned.1.call-update) | async-done | bytes 6291472 | tf_op jit(solution)/shard_map/all_gather | solution.py:36
  95.7 10.6 %copy.41 = bf16[2048,3,4,128]{0,3,2,1:T(8,128)(2,1)} copy(bf16[2048,3,4,128]{3,2,1,0:T(4,128)(2,1)} %all-gather.10.cloned.1.call-done) | data formatting | bytes 12582912 | tf_op jit(solution)/shard_map/reshape | solution.py:39
  106.3 6.2 %fusion.20 = f32[384,3,4,128]{0,3,2,1:T(8,128)S(1)} fusion(bf16[2048,3,4,128]{0,3,2,1:T(8,128)(2,1)} %copy.41, bf16[384,2048]{1,0:T(8,128)(2,1)} %all-gather.8.cloned.1.call-done, f32[2048]{0:T(1024)S(1)} %copy-done.2, f32[384]{0:T(512)S(1)} %add_rsqrt_fusion), kind=kOutput, calls=%fused_computation.25 | convolution fusion | flops 2419064832 | bytes 10233344 | tf_op jit(solution)/shard_map/dot_general | solution.py:38
  112.8 0.8 pad_maximum_fusion
  113.7 0.8 slice.47
  115.5 31.2 %all-gather.12.cloned.1.call-done = bf16[3072,4,128]{0,2,1:T(8,128)(2,1)} async-done(((bf16[384,4,128]{0,2,1:T(8,128)(2,1)}), bf16[3072,4,128]{0,2,1:T(8,128)(2,1)}) %all-gather.12.cloned.1.call-update) | async-done | bytes 3145744 | tf_op jit(solution)/shard_map/all_gather | solution.py:78
  146.6 35.1 %all-gather.18.cloned.1.call-done = bf16[3072,1,4,128]{0,3,2,1:T(8,128)(2,1)} async-done(((bf16[384,1,4,128]{0,3,2,1:T(8,128)(2,1)}), bf16[3072,1,4,128]{0,3,2,1:T(8,128)(2,1)}) %all-gather.18.cloned.1.call-update) | async-done | bytes 3145744 | tf_op jit(solution)/shard_map/all_gather | solution.py:79
  181.8 50.4 %while.18 = (s32[]{:T(128)}, f32[4,384]{1,0:T(4,128)S(1)}, f32[4,384]{1,0:T(4,128)S(1)}, f32[4,384,128]{2,1,0:T(8,128)}, s32[384]{0:T(512)S(1)}, /*index=5*/bf16...) while((s32[]{:T(128)}, f32[4,384]{1,0:T(4,128)S(1)}, ...), condition=%wide.region_6.7_spmd.clone, body=%wide.region_3.6_spmd.clone.sunk | while | flops 620798592 | bytes 37858016 | solution.py:89
  182.1 4.4 %fusion.42 = (f32[4,384]{1,0:T(4,128)S(1)}, f32[4,768,384]{2,1,0:T(8,128)}) fusion(pred[384,768]{0,1:T(8,128)(4,1)S(1)} %compare_and_fusion.2, bf16[384,4,128]{2,0,1:T(8,128)(2,1)S(1)} %get-tuple-element.368, bf16[3072,4,128]{0,2,1:T(8,128)(2,1)} %get-tuple-element.367, s32[]{:T(128)S(6)} %select_n.63), kind=kOutput, calls=%fused_computation.3.clone.1 | convolution fusion | flops 305527296 | bytes 6199300 | tf_op jit(solution)/shard_map/while/body/eval_jaxpr/qhd,khd->hqk/dot_general | solution.py:56
  186.5 3.7 %fusion.43 = f32[4,384]{1,0:T(4,128)S(1)} fusion(f32[4,768,384]{2,1,0:T(8,128)} %get-tuple-element.333, f32[4,384]{1,0:T(4,128)S(1)} %select_maximum_fusion.2, pred[384,768]{0,1:T(8,128)(4,1)S(1)} %compare_and_fusion.2), kind=kLoop, calls=%fused_computation.5.clone.1 | loop fusion | flops 5896704 | bytes 5025792 | tf_op jit(solution)/shard_map/while/body/eval_jaxpr/reduce_sum | solution.py:63
  190.3 3.9 %fusion.45 = f32[4,384,128]{2,1,0:T(8,128)} fusion(f32[4,768,384]{2,1,0:T(8,128)S(1)} %copy-done, f32[4,384]{1,0:T(4,128)S(1)} %select_maximum_fusion.2, pred[384,768]{0,1:T(8,128)(4,1)S(1)} %compare_and_fusion.2, f32[4,384,128]{2,1,0:T(8,128)} %get-tuple-element.352, bf16[3072,4,128]{0,2,1:T(8,128)(2,1)} %get-tuple-element.369, s32[]{:T(128)S(6)} %select_n.63, ...), kind=kOutput, calls=%fused_computation.8.clone.1 | convolution fusion | flops 308477952 | bytes 7385093 | tf_op jit(solution)/shard_map/while/body/eval_jaxpr/hqk,khd->hqd/dot_general | solution.py:64
  194.5 4.4 %fusion.42 = (f32[4,384]{1,0:T(4,128)S(1)}, f32[4,768,384]{2,1,0:T(8,128)}) fusion(pred[384,768]{0,1:T(8,128)(4,1)S(1)} %compare_and_fusion.2, bf16[384,4,128]{2,0,1:T(8,128)(2,1)S(1)} %get-tuple-element.368, bf16[3072,4,128]{0,2,1:T(8,128)(2,1)} %get-tuple-element.367, s32[]{:T(128)S(6)} %select_n.63), kind=kOutput, calls=%fused_computation.3.clone.1 | convolution fusion | flops 305527296 | bytes 6199300 | tf_op jit(solution)/shard_map/while/body/eval_jaxpr/qhd,khd->hqk/dot_general | solution.py:56
  198.9 3.7 %fusion.43 = f32[4,384]{1,0:T(4,128)S(1)} fusion(f32[4,768,384]{2,1,0:T(8,128)} %get-tuple-element.333, f32[4,384]{1,0:T(4,128)S(1)} %select_maximum_fusion.2, pred[384,768]{0,1:T(8,128)(4,1)S(1)} %compare_and_fusion.2), kind=kLoop, calls=%fused_computation.5.clone.1 | loop fusion | flops 5896704 | bytes 5025792 | tf_op jit(solution)/shard_map/while/body/eval_jaxpr/reduce_sum | solution.py:63
  203.0 4.1 %fusion.45 = f32[4,384,128]{2,1,0:T(8,128)} fusion(f32[4,768,384]{2,1,0:T(8,128)S(1)} %copy-done, f32[4,384]{1,0:T(4,128)S(1)} %select_maximum_fusion.2, pred[384,768]{0,1:T(8,128)(4,1)S(1)} %compare_and_fusion.2, f32[4,384,128]{2,1,0:T(8,128)} %get-tuple-element.352, bf16[3072,4,128]{0,2,1:T(8,128)(2,1)} %get-tuple-element.369, s32[]{:T(128)S(6)} %select_n.63, ...), kind=kOutput, calls=%fused_computation.8.clone.1 | convolution fusion | flops 308477952 | bytes 7385093 | tf_op jit(solution)/shard_map/while/body/eval_jaxpr/hqk,khd->hqd/dot_general | solution.py:64
  207.4 4.4 %fusion.42 = (f32[4,384]{1,0:T(4,128)S(1)}, f32[4,768,384]{2,1,0:T(8,128)}) fusion(pred[384,768]{0,1:T(8,128)(4,1)S(1)} %compare_and_fusion.2, bf16[384,4,128]{2,0,1:T(8,128)(2,1)S(1)} %get-tuple-element.368, bf16[3072,4,128]{0,2,1:T(8,128)(2,1)} %get-tuple-element.367, s32[]{:T(128)S(6)} %select_n.63), kind=kOutput, calls=%fused_computation.3.clone.1 | convolution fusion | flops 305527296 | bytes 6199300 | tf_op jit(solution)/shard_map/while/body/eval_jaxpr/qhd,khd->hqk/dot_general | solution.py:56
  211.8 3.7 %fusion.43 = f32[4,384]{1,0:T(4,128)S(1)} fusion(f32[4,768,384]{2,1,0:T(8,128)} %get-tuple-element.333, f32[4,384]{1,0:T(4,128)S(1)} %select_maximum_fusion.2, pred[384,768]{0,1:T(8,128)(4,1)S(1)} %compare_and_fusion.2), kind=kLoop, calls=%fused_computation.5.clone.1 | loop fusion | flops 5896704 | bytes 5025792 | tf_op jit(solution)/shard_map/while/body/eval_jaxpr/reduce_sum | solution.py:63
  215.6 4.1 %fusion.45 = f32[4,384,128]{2,1,0:T(8,128)} fusion(f32[4,768,384]{2,1,0:T(8,128)S(1)} %copy-done, f32[4,384]{1,0:T(4,128)S(1)} %select_maximum_fusion.2, pred[384,768]{0,1:T(8,128)(4,1)S(1)} %compare_and_fusion.2, f32[4,384,128]{2,1,0:T(8,128)} %get-tuple-element.352, bf16[3072,4,128]{0,2,1:T(8,128)(2,1)} %get-tuple-element.369, s32[]{:T(128)S(6)} %select_n.63, ...), kind=kOutput, calls=%fused_computation.8.clone.1 | convolution fusion | flops 308477952 | bytes 7385093 | tf_op jit(solution)/shard_map/while/body/eval_jaxpr/hqk,khd->hqd/dot_general | solution.py:64
  220.0 4.4 %fusion.42 = (f32[4,384]{1,0:T(4,128)S(1)}, f32[4,768,384]{2,1,0:T(8,128)}) fusion(pred[384,768]{0,1:T(8,128)(4,1)S(1)} %compare_and_fusion.2, bf16[384,4,128]{2,0,1:T(8,128)(2,1)S(1)} %get-tuple-element.368, bf16[3072,4,128]{0,2,1:T(8,128)(2,1)} %get-tuple-element.367, s32[]{:T(128)S(6)} %select_n.63), kind=kOutput, calls=%fused_computation.3.clone.1 | convolution fusion | flops 305527296 | bytes 6199300 | tf_op jit(solution)/shard_map/while/body/eval_jaxpr/qhd,khd->hqk/dot_general | solution.py:56
  224.4 3.7 %fusion.43 = f32[4,384]{1,0:T(4,128)S(1)} fusion(f32[4,768,384]{2,1,0:T(8,128)} %get-tuple-element.333, f32[4,384]{1,0:T(4,128)S(1)} %select_maximum_fusion.2, pred[384,768]{0,1:T(8,128)(4,1)S(1)} %compare_and_fusion.2), kind=kLoop, calls=%fused_computation.5.clone.1 | loop fusion | flops 5896704 | bytes 5025792 | tf_op jit(solution)/shard_map/while/body/eval_jaxpr/reduce_sum | solution.py:63
  228.1 4.1 %fusion.45 = f32[4,384,128]{2,1,0:T(8,128)} fusion(f32[4,768,384]{2,1,0:T(8,128)S(1)} %copy-done, f32[4,384]{1,0:T(4,128)S(1)} %select_maximum_fusion.2, pred[384,768]{0,1:T(8,128)(4,1)S(1)} %compare_and_fusion.2, f32[4,384,128]{2,1,0:T(8,128)} %get-tuple-element.352, bf16[3072,4,128]{0,2,1:T(8,128)(2,1)} %get-tuple-element.369, s32[]{:T(128)S(6)} %select_n.63, ...), kind=kOutput, calls=%fused_computation.8.clone.1 | convolution fusion | flops 308477952 | bytes 7385093 | tf_op jit(solution)/shard_map/while/body/eval_jaxpr/hqk,khd->hqd/dot_general | solution.py:64
  232.2 1.4 copy.36
  233.7 0.8 divide_convert_fusion
  234.5 1.0 copy.37
  235.5 1.0 copy.38
  236.5 35.2 %all-gather.14.cloned.1.call-done = bf16[384,2048]{0,1:T(8,128)(2,1)} async-done(((bf16[384,512]{0,1:T(8,128)(2,1)}), bf16[384,2048]{0,1:T(8,128)(2,1)}) %all-gather.14.cloned.1.call-update) | async-done | bytes 1572880 | tf_op jit(solution)/shard_map/all_gather | solution.py:92
  271.7 3.8 %convolution_convert_fusion = bf16[384,512]{1,0:T(8,128)(2,1)} fusion(bf16[384,2048]{0,1:T(8,128)(2,1)} %all-gather.14.cloned.1.call-done, bf16[2048,512]{1,0:T(8,128)(2,1)} %all-gather.16.cloned.1.call-done), kind=kOutput, calls=%fused_computation.35 | convolution fusion | flops 805502976 | bytes 4063232 | tf_op jit(solution)/shard_map/dot_general | solution.py:94
  (61 shorter events, 4.0 us)
Async XLA Ops:
  7.2 42.2 %all-gather.8.cloned.1.call-start = ((), (), s32[]{:S(2)}) async-start(), calls=%async_computation | async-start | bytes 1966080 | tf_op jit(solution)/shard_map/all_gather | solution.py:32
  7.9 87.8 %all-gather.10.cloned.1.call-start = ((), (), s32[]{:S(2)}) async-start(), calls=%async_computation.1 | async-start | bytes 7077888 | tf_op jit(solution)/shard_map/all_gather | solution.py:36
  8.6 138.0 %all-gather.12.cloned.1.call-start = ((), (), s32[]{:S(2)}) async-start(), calls=%async_computation.2 | async-start | bytes 3538944 | tf_op jit(solution)/shard_map/all_gather | solution.py:78
  51.2 55.1 %copy-start.2 = (f32[2048]{0:T(1024)S(1)}, f32[2048]{0:T(1024)}, u32[]{:S(2)}) copy-start(f32[2048]{0:T(1024)} %param.8) | copy-start | bytes 24580
  113.6 68.1 %all-gather.18.cloned.1.call-start = ((), (), s32[]{:S(2)}) async-start(), calls=%async_computation.5 | async-start | bytes 3538944 | tf_op jit(solution)/shard_map/all_gather | solution.py:79
  114.5 122.0 %all-gather.16.cloned.1.call-start = ((), (), s32[]{:S(2)}) async-start(), calls=%async_computation.4 | async-start | bytes 2359296 | tf_op jit(solution)/shard_map/all_gather | solution.py:95
  115.1 156.6 %all-gather.14.cloned.1.call-start = ((), (), s32[]{:S(2)}) async-start(), calls=%async_computation.3 | async-start | bytes 1966080 | tf_op jit(solution)/shard_map/all_gather | solution.py:92
  186.5 3.8 %copy-start = (f32[4,768,384]{2,1,0:T(8,128)S(1)}, f32[4,768,384]{2,1,0:T(8,128)}, u32[]{:S(2)}) copy-start(f32[4,768,384]{2,1,0:T(8,128)} %get-tuple-element.333) | copy-start | bytes 14155780 | tf_op jit(solution)/shard_map/while
  198.9 4.1 %copy-start = (f32[4,768,384]{2,1,0:T(8,128)S(1)}, f32[4,768,384]{2,1,0:T(8,128)}, u32[]{:S(2)}) copy-start(f32[4,768,384]{2,1,0:T(8,128)} %get-tuple-element.333) | copy-start | bytes 14155780 | tf_op jit(solution)/shard_map/while
  211.8 3.8 %copy-start = (f32[4,768,384]{2,1,0:T(8,128)S(1)}, f32[4,768,384]{2,1,0:T(8,128)}, u32[]{:S(2)}) copy-start(f32[4,768,384]{2,1,0:T(8,128)} %get-tuple-element.333) | copy-start | bytes 14155780 | tf_op jit(solution)/shard_map/while
  224.4 3.8 %copy-start = (f32[4,768,384]{2,1,0:T(8,128)S(1)}, f32[4,768,384]{2,1,0:T(8,128)}, u32[]{:S(2)}) copy-start(f32[4,768,384]{2,1,0:T(8,128)} %get-tuple-element.333) | copy-start | bytes 14155780 | tf_op jit(solution)/shard_map/while
  232.2 2.3 copy-start.1
Sparse Core Ops, SparseCore 0:
  9.6 39.7 all-gather.7
  51.3 44.3 all-gather.9
  113.8 32.8 all-gather.11
  148.9 32.8 all-gather.17
  183.5 27.8 all-gather.15
  234.6 37.0 all-gather.13
where the time goes:
time: 283 us; the launch traced here: 282 us
  waiting for transfers between devices  187 us (66%)
  matrix products  43.8 us (15%)
  other arithmetic  21.6 us (8%)
  local copies, waits for them, and re-layouts  15.8 us (6%)
  between operations  14.2 us (5%)
    all_gather x1, waiting for transfers between devices, local(): piece = lax.all_gather(w_qkv, 'gx', axis=0, tiled=True)  44.5 us
    all_gather x1, waiting for transfers between devices, local(): whole = lax.all_gather(tokens, 'gy', axis=1, tiled=True)  38.7 us
    all_gather x1, waiting for transfers between devices, local(): all_heads = lax.all_gather(attended, 'gy', axis=1, tiled=True)  35.2 us
    all_gather x1, waiting for transfers between devices, local(): vals_piece = lax.all_gather(vals_own, 'gx', axis=0, tiled=True)  35.1 us
    all_gather x1, waiting for transfers between devices, local(): keys_piece = lax.all_gather(keys_own, 'gx', axis=0, tiled=True)  31.2 us
    dot_general x4, matrix products, tile_step(): jnp.einsum('qhd,khd->hqk', query, keys_blk, preferred_element_type=jnp.fl...  17.7 us
    dot_general x4, matrix products, tile_step(): jnp.einsum('hqk,khd->hqd', weight.astype(jnp.bfloat16), vals_blk, preferr...  16.1 us
    reduce_sum x4, other arithmetic, tile_step(): totals = totals * factor + jnp.sum(weight, axis=-1)  14.6 us
  transfers between devices with their start and end apart: 6, of which 5 were waited for; matrix products, arithmetic and copies ran while one was open for 21% of the time, Pallas kernels for 0%

commit v1 on v0

--- a/solution.py
+++ b/solution.py
@@ -29,7 +29,16 @@
     tok_dev = tokens.shape[0]
     hloc = w_qkv.shape[2]
     hsize = w_qkv.shape[3]
-    whole = lax.all_gather(tokens, "gy", axis=1, tiled=True)
+    size_2, index, rows = (lax.axis_size("gy"), lax.axis_index("gy"), tokens.shape[1])
+    right = [(i, (i + 1) % size_2) for i in range(size_2)]
+    out = jnp.zeros((*tokens.shape[:1], size_2 * rows, *tokens.shape[1 + 1 :]), tokens.dtype)
+    held = tokens
+    for lap in range(size_2):
+        source = (index - lap) % size_2
+        out = lax.dynamic_update_slice_in_dim(out, held, source * rows, axis=1)
+        if lap < size_2 - 1:
+            held = lax.ppermute(held, "gy", right)
+    whole = out
     wide = whole.astype(jnp.float32)
     meansq = jnp.mean(wide * wide, axis=-1, keepdims=True)
     normed = (wide * lax.rsqrt(meansq + 1e-06) * gain[None, :]).astype(jnp.bfloat16)

time: 283 us -> 241 us (0.85)
  waiting for transfers between devices: 187 us -> 144 us
  matrix products: 43.8 us -> 39.8 us
  local copies, waits for them, and re-layouts: 15.8 us -> 19.1 us
  starting transfers between devices: 0.24 us -> 3.28 us
    all_gather x1 -> x0, waiting for transfers between devices: 38.7 us -> none  [local(): whole = lax.all_gather(tokens, 'gy', axis=1, tiled=True)]
    all_gather x1, waiting for transfers between devices: 44.5 us -> 12 us  [local(): piece = lax.all_gather(w_qkv, 'gx', axis=0, tiled=True)]
    ppermute x0 -> x3, waiting for transfers between devices: none -> 31.2 us  [local(): held = lax.ppermute(held, 'gy', right)]
    dot_general x4, matrix products: 16.1 us -> 12.6 us  [tile_step(): jnp.einsum('hqk,khd->hqd', weight.astype(jnp.bfloat16), vals_blk, preferr...]
    ppermute x0 -> x3, starting transfers between devices: none -> 3.08 us  [local(): held = lax.ppermute(held, 'gy', right)]
  transfers between devices with their start and end apart: 6 -> 8, of which waited for: 5 -> 7; matrix products, arithmetic and copies ran while one was open for 21% -> 23% of each run, Pallas kernels for 0% -> 0%
where the time goes in v1:
time: 241 us
  waiting for transfers between devices  144 us (60%)
  matrix products  39.8 us (17%)
  other arithmetic  20.2 us (8%)
  local copies, waits for them, and re-layouts  19.1 us (8%)
  between operations  14 us (6%)
  starting transfers between devices  3.28 us (1%)
    all_gather x1, waiting for transfers between devices, local(): vals_piece = lax.all_gather(vals_own, 'gx', axis=0, tiled=True)  35.3 us
    all_gather x1, waiting for transfers between devices, local(): all_heads = lax.all_gather(attended, 'gy', axis=1, tiled=True)  34.2 us
    ppermute x3, waiting for transfers between devices, local(): held = lax.ppermute(held, 'gy', right)  31.2 us
    all_gather x1, waiting for transfers between devices, local(): keys_piece = lax.all_gather(keys_own, 'gx', axis=0, tiled=True)  30 us
    dot_general x4, matrix products, tile_step(): jnp.einsum('qhd,khd->hqk', query, keys_blk, preferred_element_type=jnp.fl...  17.6 us
    reduce_sum x4, other arithmetic, tile_step(): totals = totals * factor + jnp.sum(weight, axis=-1)  14.6 us
    dot_general x4, matrix products, tile_step(): jnp.einsum('hqk,khd->hqd', weight.astype(jnp.bfloat16), vals_blk, preferr...  12.6 us
    all_gather x1, waiting for transfers between devices, local(): piece = lax.all_gather(w_qkv, 'gx', axis=0, tiled=True)  12 us
  transfers between devices with their start and end apart: 8, of which 7 were waited for; matrix products, arithmetic and copies ran while one was open for 23% of the time, Pallas kernels for 0%

profile of v1, /device:TPU:0, one launch (start us, length us, event | category | flops | bytes accessed | tf_op | source)
XLA Modules:
  0.0 240.6 jit_solution(17509374633634083205)
XLA Ops:
  7.9 3.1 %collective-permute-start = (bf16[384,512]{1,0:T(8,128)(2,1)}, bf16[384,512]{1,0:T(8,128)(2,1)S(1)}, u32[]{:S(2)}, u32[]{:S(2)}) collective-permute-start(bf16[384,512]{1,0:T(8,128)(2,1)} %param.7), channel_id=1, source_target_pairs={{0,1},{1,2},{2,3},{3,0},{4,5},{5,6},{6,7},{7,4},{8,9},{9,10},{10,1... | collective-permute-start | bytes 1179656 | tf_op jit(solution)/shard_map/ppermute | solution.py:40
  11.0 0.8 reduce-window.9
  12.5 9.9 %collective-permute-done = bf16[384,512]{1,0:T(8,128)(2,1)S(1)} collective-permute-done((bf16[384,512]{1,0:T(8,128)(2,1)}, bf16[384,512]{1,0:T(8,128)(2,1)S(1)}, u32[]{:S(2)}, u32[]{:S(2)}) %collective-permute-start) | collective-permute-done | bytes 393248 | tf_op jit(solution)/shard_map/ppermute | solution.py:40
  22.5 12.0 %collective-permute-done.1 = bf16[384,512]{1,0:T(8,128)(2,1)S(1)} collective-permute-done((bf16[384,512]{1,0:T(8,128)(2,1)S(1)}, bf16[384,512]{1,0:T(8,128)(2,1)S(1)}, u32[]{:S(2)}, u32[]{:S(2)}) %collective-permute-start.1) | collective-permute-done | bytes 393248 | tf_op jit(solution)/shard_map/ppermute | solution.py:40
  35.2 1.0 constant_dynamic-update-slice_fusion.3
  36.3 9.3 %collective-permute-done.2 = bf16[384,512]{1,0:T(8,128)(2,1)S(1)} collective-permute-done((bf16[384,512]{1,0:T(8,128)(2,1)S(1)}, bf16[384,512]{1,0:T(8,128)(2,1)S(1)}, u32[]{:S(2)}, u32[]{:S(2)}) %collective-permute-start.2) | collective-permute-done | bytes 393248 | tf_op jit(solution)/shard_map/ppermute | solution.py:40
  46.1 12.0 %all-gather.7.cloned.1.call-done = bf16[2048,3,4,128]{3,2,1,0:T(4,128)(2,1)} async-done(((bf16[256,3,4,128]{3,2,1,0:T(4,128)(2,1)}), bf16[2048,3,4,128]{3,2,1,0:T(4,128)(2,1)}) %all-gather.7.cloned.1.call-update) | async-done | bytes 6291472 | tf_op jit(solution)/shard_map/all_gather | solution.py:45
  58.1 10.6 %copy.41 = bf16[2048,3,4,128]{0,3,2,1:T(8,128)(2,1)} copy(bf16[2048,3,4,128]{3,2,1,0:T(4,128)(2,1)} %all-gather.7.cloned.1.call-done) | data formatting | bytes 12582912 | tf_op jit(solution)/shard_map/reshape | solution.py:48
  68.7 5.7 %fusion.20 = f32[384,3,4,128]{0,3,2,1:T(8,128)S(1)} fusion(bf16[2048,3,4,128]{0,3,2,1:T(8,128)(2,1)} %copy.41, bf16[384,2048]{1,0:T(8,128)(2,1)S(1)} %constant_dynamic-update-slice_fusion, f32[2048]{0:T(1024)S(1)} %copy-done.3, f32[384]{0:T(512)S(1)} %add_rsqrt_fusion), kind=kOutput, calls=%fused_computation.25 | convolution fusion | flops 2419064832 | bytes 10233344 | tf_op jit(solution)/shard_map/dot_general | solution.py:47
  74.8 1.2 copy-done.2
  76.8 1.9 slice.47
  79.7 30.0 %all-gather.9.cloned.1.call-done = bf16[3072,4,128]{0,2,1:T(8,128)(2,1)} async-done(((bf16[384,4,128]{0,2,1:T(8,128)(2,1)}), bf16[3072,4,128]{0,2,1:T(8,128)(2,1)}) %all-gather.9.cloned.1.call-update) | async-done | bytes 3145744 | tf_op jit(solution)/shard_map/all_gather | solution.py:87
  109.7 35.3 %all-gather.15.cloned.1.call-done = bf16[3072,1,4,128]{0,3,2,1:T(8,128)(2,1)} async-done(((bf16[384,1,4,128]{0,3,2,1:T(8,128)(2,1)}), bf16[3072,1,4,128]{0,3,2,1:T(8,128)(2,1)}) %all-gather.15.cloned.1.call-update) | async-done | bytes 3145744 | tf_op jit(solution)/shard_map/all_gather | solution.py:88
  145.0 46.8 %while.18 = (s32[]{:T(128)}, f32[4,384]{1,0:T(4,128)S(1)}, f32[4,384]{1,0:T(4,128)S(1)}, f32[4,384,128]{2,1,0:T(8,128)S(1)}, s32[384]{0:T(512)S(1)}, /*index=5*/...) while((s32[]{:T(128)}, f32[4,384]{1,0:T(4,128)S(1)}, ...), condition=%wide.region_6.7_spmd.clone, body=%wide.region_3.6_spmd.clone.sunk | while | flops 620798592 | bytes 37858016 | solution.py:98
  145.3 4.4 %fusion.42 = (f32[4,384]{1,0:T(4,128)S(1)}, f32[4,768,384]{2,1,0:T(8,128)}) fusion(pred[384,768]{0,1:T(8,128)(4,1)S(1)} %compare_and_fusion.2, bf16[384,4,128]{2,0,1:T(8,128)(2,1)S(1)} %get-tuple-element.368, bf16[3072,4,128]{0,2,1:T(8,128)(2,1)} %get-tuple-element.367, s32[]{:T(128)S(6)} %select_n.102), kind=kOutput, calls=%fused_computation.3.clone.1 | convolution fusion | flops 305527296 | bytes 6199300 | tf_op jit(solution)/shard_map/while/body/eval_jaxpr/qhd,khd->hqk/dot_general | solution.py:65
  149.8 3.7 %fusion.43 = f32[4,384]{1,0:T(4,128)S(1)} fusion(f32[4,768,384]{2,1,0:T(8,128)} %get-tuple-element.333, f32[4,384]{1,0:T(4,128)S(1)} %select_maximum_fusion.2, pred[384,768]{0,1:T(8,128)(4,1)S(1)} %compare_and_fusion.2), kind=kLoop, calls=%fused_computation.5.clone.1 | loop fusion | flops 5896704 | bytes 5025792 | tf_op jit(solution)/shard_map/while/body/eval_jaxpr/reduce_sum | solution.py:72
  153.6 3.2 %fusion.45 = f32[4,384,128]{2,1,0:T(8,128)S(1)} fusion(f32[4,768,384]{2,1,0:T(8,128)S(1)} %copy-done, f32[4,384]{1,0:T(4,128)S(1)} %select_maximum_fusion.2, pred[384,768]{0,1:T(8,128)(4,1)S(1)} %compare_and_fusion.2, f32[4,384,128]{2,1,0:T(8,128)S(1)} %get-tuple-element.352, bf16[3072,4,128]{0,2,1:T(8,128)(2,1)} %get-tuple-element.369, ...), kind=kOutput, calls=%fused_computation.8.clone.1 | convolution fusion | flops 308477952 | bytes 7385093 | tf_op jit(solution)/shard_map/while/body/eval_jaxpr/hqk,khd->hqd/dot_general | solution.py:73
  157.1 4.4 %fusion.42 = (f32[4,384]{1,0:T(4,128)S(1)}, f32[4,768,384]{2,1,0:T(8,128)}) fusion(pred[384,768]{0,1:T(8,128)(4,1)S(1)} %compare_and_fusion.2, bf16[384,4,128]{2,0,1:T(8,128)(2,1)S(1)} %get-tuple-element.368, bf16[3072,4,128]{0,2,1:T(8,128)(2,1)} %get-tuple-element.367, s32[]{:T(128)S(6)} %select_n.102), kind=kOutput, calls=%fused_computation.3.clone.1 | convolution fusion | flops 305527296 | bytes 6199300 | tf_op jit(solution)/shard_map/while/body/eval_jaxpr/qhd,khd->hqk/dot_general | solution.py:65
  161.5 3.7 %fusion.43 = f32[4,384]{1,0:T(4,128)S(1)} fusion(f32[4,768,384]{2,1,0:T(8,128)} %get-tuple-element.333, f32[4,384]{1,0:T(4,128)S(1)} %select_maximum_fusion.2, pred[384,768]{0,1:T(8,128)(4,1)S(1)} %compare_and_fusion.2), kind=kLoop, calls=%fused_computation.5.clone.1 | loop fusion | flops 5896704 | bytes 5025792 | tf_op jit(solution)/shard_map/while/body/eval_jaxpr/reduce_sum | solution.py:72
  165.3 3.1 %fusion.45 = f32[4,384,128]{2,1,0:T(8,128)S(1)} fusion(f32[4,768,384]{2,1,0:T(8,128)S(1)} %copy-done, f32[4,384]{1,0:T(4,128)S(1)} %select_maximum_fusion.2, pred[384,768]{0,1:T(8,128)(4,1)S(1)} %compare_and_fusion.2, f32[4,384,128]{2,1,0:T(8,128)S(1)} %get-tuple-element.352, bf16[3072,4,128]{0,2,1:T(8,128)(2,1)} %get-tuple-element.369, ...), kind=kOutput, calls=%fused_computation.8.clone.1 | convolution fusion | flops 308477952 | bytes 7385093 | tf_op jit(solution)/shard_map/while/body/eval_jaxpr/hqk,khd->hqd/dot_general | solution.py:73
  168.8 4.4 %fusion.42 = (f32[4,384]{1,0:T(4,128)S(1)}, f32[4,768,384]{2,1,0:T(8,128)}) fusion(pred[384,768]{0,1:T(8,128)(4,1)S(1)} %compare_and_fusion.2, bf16[384,4,128]{2,0,1:T(8,128)(2,1)S(1)} %get-tuple-element.368, bf16[3072,4,128]{0,2,1:T(8,128)(2,1)} %get-tuple-element.367, s32[]{:T(128)S(6)} %select_n.102), kind=kOutput, calls=%fused_computation.3.clone.1 | convolution fusion | flops 305527296 | bytes 6199300 | tf_op jit(solution)/shard_map/while/body/eval_jaxpr/qhd,khd->hqk/dot_general | solution.py:65
  173.2 3.7 %fusion.43 = f32[4,384]{1,0:T(4,128)S(1)} fusion(f32[4,768,384]{2,1,0:T(8,128)} %get-tuple-element.333, f32[4,384]{1,0:T(4,128)S(1)} %select_maximum_fusion.2, pred[384,768]{0,1:T(8,128)(4,1)S(1)} %compare_and_fusion.2), kind=kLoop, calls=%fused_computation.5.clone.1 | loop fusion | flops 5896704 | bytes 5025792 | tf_op jit(solution)/shard_map/while/body/eval_jaxpr/reduce_sum | solution.py:72
  177.0 3.1 %fusion.45 = f32[4,384,128]{2,1,0:T(8,128)S(1)} fusion(f32[4,768,384]{2,1,0:T(8,128)S(1)} %copy-done, f32[4,384]{1,0:T(4,128)S(1)} %select_maximum_fusion.2, pred[384,768]{0,1:T(8,128)(4,1)S(1)} %compare_and_fusion.2, f32[4,384,128]{2,1,0:T(8,128)S(1)} %get-tuple-element.352, bf16[3072,4,128]{0,2,1:T(8,128)(2,1)} %get-tuple-element.369, ...), kind=kOutput, calls=%fused_computation.8.clone.1 | convolution fusion | flops 308477952 | bytes 7385093 | tf_op jit(solution)/shard_map/while/body/eval_jaxpr/hqk,khd->hqd/dot_general | solution.py:73
  180.5 4.4 %fusion.42 = (f32[4,384]{1,0:T(4,128)S(1)}, f32[4,768,384]{2,1,0:T(8,128)}) fusion(pred[384,768]{0,1:T(8,128)(4,1)S(1)} %compare_and_fusion.2, bf16[384,4,128]{2,0,1:T(8,128)(2,1)S(1)} %get-tuple-element.368, bf16[3072,4,128]{0,2,1:T(8,128)(2,1)} %get-tuple-element.367, s32[]{:T(128)S(6)} %select_n.102), kind=kOutput, calls=%fused_computation.3.clone.1 | convolution fusion | flops 305527296 | bytes 6199300 | tf_op jit(solution)/shard_map/while/body/eval_jaxpr/qhd,khd->hqk/dot_general | solution.py:65
  184.9 3.7 %fusion.43 = f32[4,384]{1,0:T(4,128)S(1)} fusion(f32[4,768,384]{2,1,0:T(8,128)} %get-tuple-element.333, f32[4,384]{1,0:T(4,128)S(1)} %select_maximum_fusion.2, pred[384,768]{0,1:T(8,128)(4,1)S(1)} %compare_and_fusion.2), kind=kLoop, calls=%fused_computation.5.clone.1 | loop fusion | flops 5896704 | bytes 5025792 | tf_op jit(solution)/shard_map/while/body/eval_jaxpr/reduce_sum | solution.py:72
  188.7 3.1 %fusion.45 = f32[4,384,128]{2,1,0:T(8,128)S(1)} fusion(f32[4,768,384]{2,1,0:T(8,128)S(1)} %copy-done, f32[4,384]{1,0:T(4,128)S(1)} %select_maximum_fusion.2, pred[384,768]{0,1:T(8,128)(4,1)S(1)} %compare_and_fusion.2, f32[4,384,128]{2,1,0:T(8,128)S(1)} %get-tuple-element.352, bf16[3072,4,128]{0,2,1:T(8,128)(2,1)} %get-tuple-element.369, ...), kind=kOutput, calls=%fused_computation.8.clone.1 | convolution fusion | flops 308477952 | bytes 7385093 | tf_op jit(solution)/shard_map/while/body/eval_jaxpr/hqk,khd->hqd/dot_general | solution.py:73
  192.1 0.8 divide_convert_fusion
  193.0 1.0 copy.37
  193.9 1.2 slice_bitcast_fusion.2
  195.1 1.0 copy.38
  196.1 34.2 %all-gather.11.cloned.1.call-done = bf16[384,2048]{0,1:T(8,128)(2,1)} async-done(((bf16[384,512]{0,1:T(8,128)(2,1)}), bf16[384,2048]{0,1:T(8,128)(2,1)}) %all-gather.11.cloned.1.call-update) | async-done | bytes 1572880 | tf_op jit(solution)/shard_map/all_gather | solution.py:101
  230.2 3.8 %convolution_convert_fusion = bf16[384,512]{1,0:T(8,128)(2,1)} fusion(bf16[384,2048]{0,1:T(8,128)(2,1)} %all-gather.11.cloned.1.call-done, bf16[2048,512]{1,0:T(8,128)(2,1)} %all-gather.13.cloned.1.call-done), kind=kOutput, calls=%fused_computation.35 | convolution fusion | flops 805502976 | bytes 4063232 | tf_op jit(solution)/shard_map/dot_general | solution.py:103
  (71 shorter events, 6.7 us)
Async XLA Ops:
  7.2 51.0 %all-gather.7.cloned.1.call-start = ((), (), s32[]{:S(2)}) async-start(), calls=%async_computation | async-start | bytes 7077888 | tf_op jit(solution)/shard_map/all_gather | solution.py:45
  7.9 101.8 %all-gather.9.cloned.1.call-start = ((), (), s32[]{:S(2)}) async-start(), calls=%async_computation.1 | async-start | bytes 3538944 | tf_op jit(solution)/shard_map/all_gather | solution.py:87
  7.9 14.4 %collective-permute-start = (bf16[384,512]{1,0:T(8,128)(2,1)}, bf16[384,512]{1,0:T(8,128)(2,1)S(1)}, u32[]{:S(2)}, u32[]{:S(2)}) collective-permute-start(bf16[384,512]{1,0:T(8,128)(2,1)} %param.7), channel_id=1, source_target_pairs={{0,1},{1,2},{2,3},{3,0},{4,5},{5,6},{6,7},{7,4},{8,9},{9,10},{10,1... | collective-permute-start | bytes 1179656 | tf_op jit(solution)/shard_map/ppermute | solution.py:40
  22.4 12.1 %collective-permute-start.1 = (bf16[384,512]{1,0:T(8,128)(2,1)S(1)}, bf16[384,512]{1,0:T(8,128)(2,1)S(1)}, u32[]{:S(2)}, u32[]{:S(2)}) collective-permute-start(bf16[384,512]{1,0:T(8,128)(2,1)S(1)} %collective-permute-done), channel_id=1, source_target_pairs={{0,1},{1,2},{2,3},{3,0},{4,5},{5,6},{6,7},{7,4},{8,9},{9,10},{10,1... | collective-permute-start | bytes 1179656 | tf_op jit(solution)/shard_map/ppermute | solution.py:40
  34.5 11.2 %collective-permute-start.2 = (bf16[384,512]{1,0:T(8,128)(2,1)S(1)}, bf16[384,512]{1,0:T(8,128)(2,1)S(1)}, u32[]{:S(2)}, u32[]{:S(2)}) collective-permute-start(bf16[384,512]{1,0:T(8,128)(2,1)S(1)} %collective-permute-done.1), channel_id=1, source_target_pairs={{0,1},{1,2},{2,3},{3,0},{4,5},{5,6},{6,7},{7,4},{8,9},{9,10},{10,1... | collective-permute-start | bytes 1179656 | tf_op jit(solution)/shard_map/ppermute | solution.py:40
  46.1 22.6 %copy-start.3 = (f32[2048]{0:T(1024)S(1)}, f32[2048]{0:T(1024)}, u32[]{:S(2)}) copy-start(f32[2048]{0:T(1024)} %param.8) | copy-start | bytes 24580
  74.4 1.5 copy-start.2
  76.8 68.3 %all-gather.15.cloned.1.call-start = ((), (), s32[]{:S(2)}) async-start(), calls=%async_computation.4 | async-start | bytes 3538944 | tf_op jit(solution)/shard_map/all_gather | solution.py:88
  78.8 117.3 %all-gather.13.cloned.1.call-start = ((), (), s32[]{:S(2)}) async-start(), calls=%async_computation.3 | async-start | bytes 2359296 | tf_op jit(solution)/shard_map/all_gather | solution.py:104
  79.3 150.9 %all-gather.11.cloned.1.call-start = ((), (), s32[]{:S(2)}) async-start(), calls=%async_computation.2 | async-start | bytes 1966080 | tf_op jit(solution)/shard_map/all_gather | solution.py:101
  149.8 3.8 %copy-start = (f32[4,768,384]{2,1,0:T(8,128)S(1)}, f32[4,768,384]{2,1,0:T(8,128)}, u32[]{:S(2)}) copy-start(f32[4,768,384]{2,1,0:T(8,128)} %get-tuple-element.333) | copy-start | bytes 14155780 | tf_op jit(solution)/shard_map/while
  161.5 3.8 %copy-start = (f32[4,768,384]{2,1,0:T(8,128)S(1)}, f32[4,768,384]{2,1,0:T(8,128)}, u32[]{:S(2)}) copy-start(f32[4,768,384]{2,1,0:T(8,128)} %get-tuple-element.333) | copy-start | bytes 14155780 | tf_op jit(solution)/shard_map/while
  173.2 3.8 %copy-start = (f32[4,768,384]{2,1,0:T(8,128)S(1)}, f32[4,768,384]{2,1,0:T(8,128)}, u32[]{:S(2)}) copy-start(f32[4,768,384]{2,1,0:T(8,128)} %get-tuple-element.333) | copy-start | bytes 14155780 | tf_op jit(solution)/shard_map/while
  184.9 3.8 %copy-start = (f32[4,768,384]{2,1,0:T(8,128)S(1)}, f32[4,768,384]{2,1,0:T(8,128)}, u32[]{:S(2)}) copy-start(f32[4,768,384]{2,1,0:T(8,128)} %get-tuple-element.333) | copy-start | bytes 14155780 | tf_op jit(solution)/shard_map/while
  191.8 1.1 copy-start.1
Sparse Core Ops, SparseCore 0:
  9.9 48.2 all-gather.6
  76.9 32.8 all-gather.8
  112.2 32.8 all-gather.14
  146.8 27.8 all-gather.12
  193.1 37.1 all-gather.10
